TPU v7x, 32 devices: a whole 2x2x4 slice. The times are simulated.
32 devices in a mesh: grp: 4 (over y, core), dev: 8 (over z, x).
Axes of the slice: x: 2, y: 2, z: 4, core: 2. Of those that a mesh axis runs over, the one named last changes fastest.
Arguments:
- tokens: bfloat16 [4096, 2048], P(('grp', 'dev')), may hold values from -6 to 6
- cotangent: bfloat16 [4096, 2048], P(('grp', 'dev')), may hold values from -1.5 to 1.5
- route_weight: float32 [4096, 2], P(('grp', 'dev')), may hold values from 0.1 to 1
- slot_expert: int32 [32], replicated, may hold values from 0 to 15, as said below
- targets: int32 [4096, 2], P(('grp', 'dev')), may hold values from 0 to 31, as said below
- proj_in: float32 [16, 2048, 2048], P('grp', 'dev'), may hold values from -0.125 to 0.125
- first_in: float32 [16, 2048, 2048], P('grp', 'dev'), may hold values from -6 to 6
- second_in: float32 [16, 2048, 2048], P('grp', 'dev'), may hold values from 0.01 to 1
- proj_out: float32 [16, 1024, 2048], P('grp', 'dev'), may hold values from -0.1875 to 0.1875
- first_out: float32 [16, 1024, 2048], P('grp', 'dev'), may hold values from -6 to 6
- second_out: float32 [16, 1024, 2048], P('grp', 'dev'), may hold values from 0.01 to 1
Outputs:
- mixed: bfloat16 [4096, 2048], P(('grp', 'dev'))
- token_grad: bfloat16 [4096, 2048], P(('grp', 'dev'))
- mix_grad: float32 [4096, 2], P(('grp', 'dev'))
- trained_in: float32 [16, 2048, 2048], P('grp', 'dev')
- mean_in: float32 [16, 2048, 2048], P('grp', 'dev')
- square_in: float32 [16, 2048, 2048], P('grp', 'dev')
- trained_out: float32 [16, 1024, 2048], P('grp', 'dev')
- mean_out: float32 [16, 1024, 2048], P('grp', 'dev')
- square_out: float32 [16, 1024, 2048], P('grp', 'dev')
Inputs may be any that keep to these rules, and one draw needn't show every extreme that they name: `slot_expert`: entry s is the expert held by slot s, the device s in grp+dev order; each of the 16 experts is held by at least one slot. `targets`: entry [t, k] is the slot that serves the k-th expert of token t; the two slots of a token hold different experts.
All inputs are finite; a program needn't handle non-finite values.
Results may differ from a plain program's by a relative error of at most 0.015.
The roundings to bfloat16 on the way count: a program that leaves them out, or rounds other values in their place, can miss the bound.
Values may be sent and summed in bfloat16 or wider, within the bound.
A program may use at most 192 MiB of HBM per device.

v0:
```python
import jax
import jax.numpy as jnp
from jax import lax
from jax.sharding import PartitionSpec as P

D = 2048
FF = 1024
E = 16


beta_first = 0.9
beta_second = 0.95
learn_rate = 0.01
decay_rate = 0.1
adam_eps = 1e-08
bias_first = 1.0 - 0.9**10
bias_second = 1.0 - 0.95**10


def silu_parts(values):
    logistic = jax.nn.sigmoid(values)
    return (values * logistic, logistic * (1.0 + values * (1.0 - logistic)))


def slot_pass(rows_x, rows_dy, weight_up, weight_down):
    gate_up = jnp.dot(rows_x, weight_up, preferred_element_type=jnp.float32)
    gating = gate_up[:, :FF]
    upward = gate_up[:, FF:]
    active, derivative = silu_parts(gating)
    hidden = (active * upward).astype(jnp.bfloat16)
    result = jnp.dot(hidden, weight_down, preferred_element_type=jnp.float32).astype(jnp.bfloat16)
    dhidden = lax.dot_general(
        rows_dy, weight_down, (((1,), (1,)), ((), ())), preferred_element_type=jnp.float32
    )
    grad_gateup = jnp.concatenate([dhidden * upward * derivative, dhidden * active], axis=1).astype(
        jnp.bfloat16
    )
    rows_dx = lax.dot_general(
        grad_gateup, weight_up, (((1,), (1,)), ((), ())), preferred_element_type=jnp.float32
    ).astype(jnp.bfloat16)
    grad_up = lax.dot_general(
        rows_x, grad_gateup, (((0,), (0,)), ((), ())), preferred_element_type=jnp.float32
    ).astype(jnp.bfloat16)
    grad_down = lax.dot_general(
        hidden, rows_dy, (((0,), (0,)), ((), ())), preferred_element_type=jnp.float32
    ).astype(jnp.bfloat16)
    return (result, rows_dx, grad_up, grad_down)


def adam_step(weight, moment, square, gradient):
    new_moment = beta_first * moment + (1.0 - beta_first) * gradient
    new_square = beta_second * square + (1.0 - beta_second) * gradient * gradient
    update = (
        new_moment / bias_first / (jnp.sqrt(new_square / bias_second) + adam_eps)
        + decay_rate * weight
    )
    return (weight - learn_rate * update, new_moment, new_square)


def to_slots(payload_x, payload_dy):
    moved_x, moved_dy = (
        lax.all_to_all(payload_x, ("grp", "dev"), split_axis=0, concat_axis=0, tiled=True),
        lax.all_to_all(payload_dy, ("grp", "dev"), split_axis=0, concat_axis=0, tiled=True),
    )
    return (moved_x, moved_dy)


def to_sources(payload_out, payload_dx):
    moved_out, moved_dx = (
        lax.all_to_all(payload_out, ("grp", "dev"), split_axis=0, concat_axis=0, tiled=True),
        lax.all_to_all(payload_dx, ("grp", "dev"), split_axis=0, concat_axis=0, tiled=True),
    )
    return (moved_out, moved_dx)


def on_device(
    tokens,
    cotangent,
    route_weight,
    slot_expert,
    targets,
    proj_in,
    first_in,
    second_in,
    proj_out,
    first_out,
    second_out,
):
    groups = lax.axis_size("grp")
    members = lax.axis_size("dev")
    slot_count = groups * members
    tok_count = tokens.shape[0]
    assigns = 2 * tok_count
    capacity = 3 * tok_count // slot_count
    buffer_rows = slot_count * capacity
    flat_target = targets.reshape(-1)
    onehot = (flat_target[:, None] == jnp.arange(slot_count, dtype=jnp.int32)[None, :]).astype(
        jnp.int32
    )
    earlier = jnp.cumsum(onehot, axis=0) - onehot
    position = jnp.sum(earlier * onehot, axis=1)
    within = position < capacity
    dest_row = jnp.where(within, flat_target * capacity + position, buffer_rows)
    matched = dest_row[:, None] == jnp.arange(buffer_rows, dtype=jnp.int32)[None, :]
    filled = jnp.any(matched, axis=0)
    source_id = jnp.sum(
        jnp.where(matched, jnp.arange(assigns, dtype=jnp.int32)[:, None], 0), axis=0
    )
    scaled = (
        route_weight.reshape(-1)[:, None] * jnp.repeat(cotangent, 2, axis=0).astype(jnp.float32)
    ).astype(jnp.bfloat16)
    send_x = jnp.where(filled[:, None], tokens[source_id // 2], jnp.zeros((), jnp.bfloat16))
    send_dy = jnp.where(filled[:, None], scaled[source_id], jnp.zeros((), jnp.bfloat16))
    slot_x, slot_dy = to_slots(
        send_x.reshape(slot_count, capacity, D), send_dy.reshape(slot_count, capacity, D)
    )
    slot_x = slot_x.reshape(buffer_rows, D)
    slot_dy = slot_dy.reshape(buffer_rows, D)
    my_group = lax.axis_index("grp")
    group_expert = lax.dynamic_slice_in_dim(slot_expert, my_group * members, members)
    low_in = proj_in.astype(jnp.bfloat16)
    low_out = proj_out.astype(jnp.bfloat16)
    all_up, all_down = (
        lax.all_gather(low_in, "grp", axis=0, tiled=True),
        lax.all_gather(low_out, "grp", axis=0, tiled=True),
    )
    send_up = jnp.take(all_up, group_expert, axis=0)
    send_down = jnp.take(all_down, group_expert, axis=0)
    got_up, got_down = (
        lax.all_to_all(send_up, "dev", split_axis=0, concat_axis=0, tiled=True),
        lax.all_to_all(send_down, "dev", split_axis=0, concat_axis=0, tiled=True),
    )
    slot_up = got_up.reshape(D, 2 * FF)
    slot_down = got_down.reshape(FF, D)
    result, rows_dx, grad_up, grad_down = slot_pass(slot_x, slot_dy, slot_up, slot_down)
    back_out, back_dx = to_sources(
        result.reshape(slot_count, capacity, D), rows_dx.reshape(slot_count, capacity, D)
    )
    flat_out = back_out.reshape(buffer_rows, D)
    flat_dx = back_dx.reshape(buffer_rows, D)
    pick_row = jnp.where(within, flat_target * capacity + position, 0)
    assigned_out = jnp.where(
        within[:, None], flat_out[pick_row], jnp.zeros((), jnp.bfloat16)
    ).reshape(tok_count, 2, D)
    assigned_dx = jnp.where(
        within[:, None], flat_dx[pick_row], jnp.zeros((), jnp.bfloat16)
    ).reshape(tok_count, 2, D)
    out_float = assigned_out.astype(jnp.float32)
    mixed = (
        route_weight[:, 0:1] * out_float[:, 0] + route_weight[:, 1:2] * out_float[:, 1]
    ).astype(jnp.bfloat16)
    token_grad = (
        assigned_dx[:, 0].astype(jnp.float32) + assigned_dx[:, 1].astype(jnp.float32)
    ).astype(jnp.bfloat16)
    mix_grad = jnp.sum(cotangent.astype(jnp.float32)[:, None, :] * out_float, axis=2)
    rows_up, rows_down = (
        lax.all_to_all(
            grad_up.reshape(members, D // members, 2 * FF),
            "dev",
            split_axis=0,
            concat_axis=0,
            tiled=True,
        ),
        lax.all_to_all(
            grad_down.reshape(members, FF // members, D),
            "dev",
            split_axis=0,
            concat_axis=0,
            tiled=True,
        ),
    )
    holder = (group_expert[None, :] == jnp.arange(E, dtype=jnp.int32)[:, None]).astype(jnp.bfloat16)
    part_up = jnp.einsum("ed,drc->erc", holder, rows_up, preferred_element_type=jnp.float32)
    part_down = jnp.einsum("ed,drc->erc", holder, rows_down, preferred_element_type=jnp.float32)
    sum_up, sum_down = (
        lax.psum_scatter(
            part_up.astype(jnp.bfloat16), "grp", scatter_dimension=0, tiled=True
        ).astype(jnp.float32),
        lax.psum_scatter(
            part_down.astype(jnp.bfloat16), "grp", scatter_dimension=0, tiled=True
        ).astype(jnp.float32),
    )
    trained_in, mean_in, square_in = adam_step(proj_in, first_in, second_in, sum_up)
    trained_out, mean_out, square_out = adam_step(proj_out, first_out, second_out, sum_down)
    return (
        mixed,
        token_grad,
        mix_grad,
        trained_in,
        mean_in,
        square_in,
        trained_out,
        mean_out,
        square_out,
    )


def solution(mesh):
    in_specs = (
        P(("grp", "dev"), None),
        P(("grp", "dev"), None),
        P(("grp", "dev"), None),
        P(),
        P(("grp", "dev"), None),
        P("grp", "dev", None),
        P("grp", "dev", None),
        P("grp", "dev", None),
        P("grp", "dev", None),
        P("grp", "dev", None),
        P("grp", "dev", None),
    )
    out_specs = (
        P(("grp", "dev"), None),
        P(("grp", "dev"), None),
        P(("grp", "dev"), None),
        P("grp", "dev", None),
        P("grp", "dev", None),
        P("grp", "dev", None),
        P("grp", "dev", None),
        P("grp", "dev", None),
        P("grp", "dev", None),
    )
    return jax.shard_map(
        on_device, mesh=mesh, in_specs=in_specs, out_specs=out_specs, check_vma=False
    )
```

profile of v0, /device:TPU:10, one launch (start us, length us, event | category | flops | bytes accessed | tf_op | source)
XLA Modules:
  0.0 1163.2 jit_solution(7193962048250886740)
XLA Ops:
  36.6 52.4 %all_to_all.40 = bf16[32,12,2048]{2,1,0:T(8,128)(2,1)S(1)} all-to-all(bf16[32,12,2048]{2,1,0:T(8,128)(2,1)S(1)} %get-tuple-element.58), channel_id=1, replica_groups=mesh['grp'=4,'dev'=8] {'grp','dev'}, dimensions={0} | all-to-all | bytes 3145728 | tf_op jit(solution)/shard_map/all_to_all | solution.py:63
  89.1 6.7 all-to-all-start
  95.8 69.7 %all-gather.3.cloned.1.call-done = bf16[16,256,2048]{2,1,0:T(8,128)(2,1)} async-done(((bf16[4,256,2048]{2,1,0:T(8,128)(2,1)}), bf16[16,256,2048]{2,1,0:T(8,128)(2,1)}) %all-gather.3.cloned.1.call-update) | async-done | bytes 16777232 | tf_op jit(solution)/shard_map/all_gather | solution.py:124
  165.5 10.6 gather_fusion.1
  176.1 7.6 broadcast_select_fusion
  194.1 175.9 %all-to-all-done.1 = bf16[8,256,2048]{2,1,0:T(8,128)(2,1)} async-done(((bf16[8,256,2048]{2,1,0:T(8,128)(2,1)}), bf16[8,256,2048]{2,1,0:T(8,128)(2,1)}, u32[]{:S(2)}, u32[]{:S(2)}) %all-to-all-start.1) | async-done | bytes 8388640 | tf_op jit(solution)/shard_map/all_to_all | solution.py:130
  380.5 98.0 %all_to_all.41 = bf16[8,128,2048]{2,1,0:T(8,128)(2,1)S(1)} all-to-all(bf16[8,128,2048]{2,1,0:T(8,128)(2,1)S(1)} %bitcast.62), channel_id=1, replica_groups=mesh['grp'=4,'dev'=8] {'dev'}, dimensions={0} | all-to-all | bytes 8388608 | tf_op jit(solution)/shard_map/all_to_all | solution.py:164
  478.5 7.1 convolution_convert_fusion.2
  485.5 11.4 copy.87
  497.2 71.1 %reduce-scatter.5.cloned.1.call-done = bf16[4,128,2048]{2,1,0:T(8,128)(2,1)} async-done(((bf16[16,128,2048]{2,1,0:T(8,128)(2,1)}), bf16[4,128,2048]{2,1,0:T(8,128)(2,1)}) %reduce-scatter.5.cloned.1.call-update) | async-done | bytes 2097168 | tf_op jit(solution)/shard_map/reduce_scatter | solution.py:179
  568.3 12.7 %multiply_subtract_fusion.1 = (f32[4,128,2048]{2,1,0:T(8,128)}, f32[4,128,2048]{2,1,0:T(8,128)}, f32[4,128,2048]{2,1,0:T(8,128)}, bf16[4,128,2048]{2,1,0:T(8,128)(2,1)}) fusion(f32[4,128,2048]{2,1,0:T(8,128)} %param.19, bf16[4,128,2048]{2,1,0:T(8,128)(2,1)} %reduce-scatter.5.cloned.1.call-done, f32[4,128,2048]{2,1,0:T(8,128)} %param.20, ...), kind=kLoop, calls=%fused_computation.21 | loop fusion | flops 17825792 | bytes 29360128 | tf_op jit(solution)/shard_map/sub | solution.py:57
  581.1 58.3 %all-gather.5.cloned.1.call-done = bf16[16,128,2048]{2,1,0:T(8,128)(2,1)} async-done(((bf16[4,128,2048]{2,1,0:T(8,128)(2,1)}), bf16[16,128,2048]{2,1,0:T(8,128)(2,1)}) %all-gather.5.cloned.1.call-update) | async-done | bytes 8388624 | tf_op jit(solution)/shard_map/all_gather | solution.py:125
  639.4 6.2 gather_fusion.2
  648.3 97.5 %all_to_all.42 = bf16[8,128,2048]{2,1,0:T(8,128)(2,1)S(1)} all-to-all(bf16[8,128,2048]{2,1,0:T(8,128)(2,1)S(1)} %broadcast_select_fusion.1), channel_id=1, replica_groups=mesh['grp'=4,'dev'=8] {'dev'}, dimensions={0} | all-to-all | bytes 8388608 | tf_op jit(solution)/shard_map/all_to_all | solution.py:131
  753.1 186.8 %all_to_all.43 = bf16[8,256,2048]{2,1,0:T(8,128)(2,1)} all-to-all(bf16[8,256,2048]{2,1,0:T(8,128)(2,1)S(1)} %bitcast.59), channel_id=1, replica_groups=mesh['grp'=4,'dev'=8] {'dev'}, dimensions={0} | all-to-all | bytes 16777216 | tf_op jit(solution)/shard_map/all_to_all | solution.py:157
  939.9 16.1 %convolution_convert_fusion = bf16[16,256,2048]{2,0,1:T(8,128)(2,1)S(1)} fusion(bf16[8,256,2048]{2,1,0:T(8,128)(2,1)} %all_to_all.43, s32[8]{0:T(128)S(1)} %get-tuple-element.54), kind=kOutput, calls=%fused_computation.6 | convolution fusion | flops 142606464 | bytes 25165856 | tf_op jit(solution)/shard_map/ed,drc->erc/dot_general | solution.py:173
  956.0 20.9 %copy.85 = bf16[16,256,2048]{2,1,0:T(8,128)(2,1)} copy(bf16[16,256,2048]{2,0,1:T(8,128)(2,1)S(1)} %convolution_convert_fusion) | data formatting | bytes 33554432 | tf_op jit(solution)/shard_map/convert_element_type | solution.py:177
  977.0 7.3 convolution_convert_fusion.4
  991.1 6.3 convolution_convert_fusion.5
  1001.2 36.0 %all-to-all-done.5 = bf16[32,12,2048]{2,1,0:T(8,128)(2,1)S(1)} async-done(((bf16[32,12,2048]{2,1,0:T(8,128)(2,1)}), bf16[32,12,2048]{2,1,0:T(8,128)(2,1)S(1)}, u32[]{:S(2)}, u32[]{:S(2)}) %all-to-all-start.5) | async-done | bytes 1572896 | tf_op jit(solution)/shard_map/all_to_all | solution.py:71
  1037.2 7.1 all-to-all-start.3
  1050.4 40.2 %all-to-all-done.3 = bf16[32,12,2048]{2,1,0:T(8,128)(2,1)} async-done(((bf16[32,12,2048]{2,1,0:T(8,128)(2,1)}), bf16[32,12,2048]{2,1,0:T(8,128)(2,1)}, u32[]{:S(2)}, u32[]{:S(2)}) %all-to-all-start.3) | async-done | bytes 1572896 | tf_op jit(solution)/shard_map/all_to_all | solution.py:70
  1103.6 32.5 %reduce-scatter.3.cloned.1.call-done = bf16[4,256,2048]{2,1,0:T(8,128)(2,1)} async-done(((bf16[16,256,2048]{2,1,0:T(8,128)(2,1)}), bf16[4,256,2048]{2,1,0:T(8,128)(2,1)}) %reduce-scatter.3.cloned.1.call-update) | async-done | bytes 4194320 | tf_op jit(solution)/shard_map/reduce_scatter | solution.py:176
  1136.1 20.1 %multiply_subtract_fusion = (f32[4,256,2048]{2,1,0:T(8,128)}, f32[4,256,2048]{2,1,0:T(8,128)}, f32[4,256,2048]{2,1,0:T(8,128)}) fusion(f32[4,256,2048]{2,1,0:T(8,128)} %param.16, bf16[4,256,2048]{2,1,0:T(8,128)(2,1)} %reduce-scatter.3.cloned.1.call-done, f32[4,256,2048]{2,1,0:T(8,128)} %param.17, f32[4,256,2048]{2,1,0:T(8,128)} %param.18), kind=kLoop, calls=%fused_computation.12 | loop fusion | flops 33554432 | bytes 54525952 | tf_op jit(solution)/shard_map/sub | solution.py:57
  (103 shorter events, 89.9 us)
Async XLA Ops:
  7.2 8.9 copy-start
  7.2 158.3 %all-gather.3.cloned.1.call-start = ((), (), s32[]{:S(2)}) async-start(), calls=%async_computation.10 | async-start | bytes 20971520 | tf_op jit(solution)/shard_map/all_gather | solution.py:124
  13.3 0.7 copy-start.11
  13.3 2.3 copy-start.12
  16.1 4.0 copy-start.10
  28.8 4.4 copy-start.3
  36.6 59.1 %copy-start.13 = (s32[32]{0:T(128)S(1)}, s32[32]{0:T(128)}, u32[]{:S(2)}) copy-start(s32[32]{0:T(128)} %param.14) | copy-start | bytes 388
  89.1 94.7 %all-to-all-start = ((bf16[32,12,2048]{2,1,0:T(8,128)(2,1)}), bf16[32,12,2048]{2,1,0:T(8,128)(2,1)}, u32[]{:S(2)}, u32[]{:S(2)}) async-start(bf16[32,12,2048]{2,1,0:T(8,128)(2,1)} %get-tuple-element.59), calls=%async_computation | async-start | bytes 4194304 | tf_op jit(solution)/shard_map/all_to_all | solution.py:62
  183.8 186.2 %all-to-all-start.1 = ((bf16[8,256,2048]{2,1,0:T(8,128)(2,1)}), bf16[8,256,2048]{2,1,0:T(8,128)(2,1)}, u32[]{:S(2)}, u32[]{:S(2)}) async-start(bf16[8,256,2048]{2,1,0:T(8,128)(2,1)} %broadcast_select_fusion), calls=%async_computation.1 | async-start | bytes 16777216 | tf_op jit(solution)/shard_map/all_to_all | solution.py:130
  189.8 378.5 %reduce-scatter.5.cloned.1.call-start = ((), (), s32[]{:S(2)}) async-start(), calls=%async_computation.13 | async-start | bytes 10485760 | tf_op jit(solution)/shard_map/reduce_scatter | solution.py:179
  370.0 8.1 copy-start.8
  375.9 1.7 copy-start.6
  497.0 142.4 %all-gather.5.cloned.1.call-start = ((), (), s32[]{:S(2)}) async-start(), calls=%async_computation.11 | async-start | bytes 10485760 | tf_op jit(solution)/shard_map/all_gather | solution.py:125
  581.0 555.0 %reduce-scatter.3.cloned.1.call-start = ((), (), s32[]{:S(2)}) async-start(), calls=%async_computation.12 | async-start | bytes 20971520 | tf_op jit(solution)/shard_map/reduce_scatter | solution.py:176
  648.3 97.5 %copy-start.7 = (f32[384,2048]{1,0:T(8,128)S(1)}, f32[384,2048]{1,0:T(8,128)}, u32[]{:S(2)}) copy-start(f32[384,2048]{1,0:T(8,128)} %copy-done.6) | copy-start | bytes 9437188
  648.3 97.5 %copy-start.9 = (bf16[384,2048]{1,0:T(8,128)(2,1)S(1)}, bf16[384,2048]{1,0:T(8,128)(2,1)}, u32[]{:S(2)}) copy-start(bf16[384,2048]{1,0:T(8,128)(2,1)} %reshape.242) | copy-start | bytes 4718596
  745.8 2.3 copy-start.4
  748.1 5.0 copy-start.14
  748.2 5.0 copy-start.15
  985.8 51.4 %all-to-all-start.5 = ((bf16[32,12,2048]{2,1,0:T(8,128)(2,1)}), bf16[32,12,2048]{2,1,0:T(8,128)(2,1)S(1)}, u32[]{:S(2)}, u32[]{:S(2)}) async-start(bf16[32,12,2048]{2,1,0:T(8,128)(2,1)} %reshape.243), calls=%async_computation.5 | async-start | bytes 4194304 | tf_op jit(solution)/shard_map/all_to_all | solution.py:71
  1037.2 7.7 copy-start.2
  1037.2 53.4 %all-to-all-start.3 = ((bf16[32,12,2048]{2,1,0:T(8,128)(2,1)}), bf16[32,12,2048]{2,1,0:T(8,128)(2,1)}, u32[]{:S(2)}, u32[]{:S(2)}) async-start(bf16[32,12,2048]{2,1,0:T(8,128)(2,1)} %reshape.240), calls=%async_computation.3 | async-start | bytes 4194304 | tf_op jit(solution)/shard_map/all_to_all | solution.py:70
  1094.6 4.5 copy-start.5
  1136.1 20.1 %copy-start.1 = (bf16[128,2048]{1,0:T(8,128)(2,1)S(1)}, bf16[128,2048]{1,0:T(8,128)(2,1)}, u32[]{:S(2)}) copy-start(bf16[128,2048]{1,0:T(8,128)(2,1)} %param.11) | copy-start | bytes 1572868
Sparse Core Ops, SparseCore 0:
  13.5 151.9 all-gather.2
  497.1 71.1 reduce-scatter.4
  581.1 58.2 all-gather.4
  977.1 158.9 reduce-scatter.2
where the time goes:
time: 1170 us; the launch traced here: 1160 us
  waiting for transfers between devices  484 us (41%)
  blocking collectives  435 us (37%)
  local copies, waits for them, and re-layouts  88.7 us (8%)
  other arithmetic  63.1 us (5%)
  matrix products  52.4 us (4%)
  starting transfers between devices  25.9 us (2%)
  between operations  14.6 us (1%)
    all_to_all x1, blocking collectives, on_device(): lax.all_to_all(grad_up.reshape(members, D // members, 2 * FF), 'dev', spl...  187 us
    all_to_all x1, waiting for transfers between devices, on_device(): lax.all_to_all(send_up, 'dev', split_axis=0, concat_axis=0, tiled=True)  176 us
    all_to_all x1, blocking collectives, on_device(): lax.all_to_all(grad_down.reshape(members, FF // members, D), 'dev', split...  98 us
    all_to_all x1, blocking collectives, on_device(): lax.all_to_all(send_down, 'dev', split_axis=0, concat_axis=0, tiled=True)  97.5 us
    reduce_scatter x1, waiting for transfers between devices, on_device(): lax.psum_scatter(part_down.astype(jnp.bfloat16), 'grp', scatter_dimension...  71.1 us
    all_gather x1, waiting for transfers between devices, on_device(): lax.all_gather(low_in, 'grp', axis=0, tiled=True)  69.7 us
    all_gather x1, waiting for transfers between devices, on_device(): lax.all_gather(low_out, 'grp', axis=0, tiled=True)  58.3 us
    all_to_all x1, blocking collectives, to_slots(): lax.all_to_all(payload_dy, ('grp', 'dev'), split_axis=0, concat_axis=0, t...  52.4 us
  transfers between devices with their start and end apart: 8, of which 7 were waited for; matrix products, arithmetic and copies ran while one was open for 7% of the time, Pallas kernels for 0%

commit v1 on v0

v1 whole, which is shorter than its diff:
```python
import jax
import jax.numpy as jnp
from jax import lax
from jax.experimental import pallas as pl
from jax.experimental.pallas import tpu as pltpu
from jax.sharding import PartitionSpec as P

D = 2048
FF = 1024
E = 16


beta_first = 0.9
beta_second = 0.95
learn_rate = 0.01
decay_rate = 0.1
adam_eps = 1e-08
bias_first = 1.0 - 0.9**10
bias_second = 1.0 - 0.95**10


def silu_parts(values):
    logistic = jax.nn.sigmoid(values)
    return (values * logistic, logistic * (1.0 + values * (1.0 - logistic)))


def slot_pass(rows_x, rows_dy, weight_up, weight_down):
    gate_up = jnp.dot(rows_x, weight_up, preferred_element_type=jnp.float32)
    gating = gate_up[:, :FF]
    upward = gate_up[:, FF:]
    active, derivative = silu_parts(gating)
    hidden = (active * upward).astype(jnp.bfloat16)
    result = jnp.dot(hidden, weight_down, preferred_element_type=jnp.float32).astype(jnp.bfloat16)
    dhidden = lax.dot_general(
        rows_dy, weight_down, (((1,), (1,)), ((), ())), preferred_element_type=jnp.float32
    )
    grad_gateup = jnp.concatenate([dhidden * upward * derivative, dhidden * active], axis=1).astype(
        jnp.bfloat16
    )
    rows_dx = lax.dot_general(
        grad_gateup, weight_up, (((1,), (1,)), ((), ())), preferred_element_type=jnp.float32
    ).astype(jnp.bfloat16)
    grad_up = lax.dot_general(
        rows_x, grad_gateup, (((0,), (0,)), ((), ())), preferred_element_type=jnp.float32
    ).astype(jnp.bfloat16)
    grad_down = lax.dot_general(
        hidden, rows_dy, (((0,), (0,)), ((), ())), preferred_element_type=jnp.float32
    ).astype(jnp.bfloat16)
    return (result, rows_dx, grad_up, grad_down)


def adam_step(weight, moment, square, gradient):
    new_moment = beta_first * moment + (1.0 - beta_first) * gradient
    new_square = beta_second * square + (1.0 - beta_second) * gradient * gradient
    update = (
        new_moment / bias_first / (jnp.sqrt(new_square / bias_second) + adam_eps)
        + decay_rate * weight
    )
    return (weight - learn_rate * update, new_moment, new_square)


def after(value, *earlier):
    return lax.optimization_barrier((value,) + earlier)[0]


def expert_sums(experts, rows):
    members, depth, width = rows.shape
    tile = 16

    def kernel(expert_ref, rows_ref, out_ref, acc_ref):
        acc_ref[...] = jnp.zeros_like(acc_ref)

        def add(d, carry):
            e = expert_ref[d]
            acc_ref[e] = acc_ref[e] + rows_ref[d].astype(jnp.float32)
            return carry

        lax.fori_loop(0, members, add, 0)
        out_ref[...] = acc_ref[...].astype(out_ref.dtype)

    return pl.pallas_call(
        kernel,
        grid_spec=pltpu.PrefetchScalarGridSpec(
            num_scalar_prefetch=1,
            grid=(depth // tile,),
            in_specs=[pl.BlockSpec((members, tile, width), lambda i, e: (0, i, 0))],
            out_specs=pl.BlockSpec((E, tile, width), lambda i, e: (0, i, 0)),
            scratch_shapes=[pltpu.VMEM((E, tile, width), jnp.float32)],
        ),
        out_shape=jax.ShapeDtypeStruct((E, depth, width), jnp.bfloat16),
        compiler_params=pltpu.CompilerParams(vmem_limit_bytes=24 * 1024 * 1024),
        cost_estimate=pl.CostEstimate(
            flops=members * depth * width,
            bytes_accessed=2 * (members + E) * depth * width,
            transcendentals=0,
        ),
    )(experts, rows)


def pick_experts(stack, experts):
    return jnp.take(stack, experts, axis=0, mode="clip")


def exchange(payload, axes):
    return lax.all_to_all(payload, axes, split_axis=0, concat_axis=0, tiled=True)


def on_device(
    tokens,
    cotangent,
    route_weight,
    slot_expert,
    targets,
    proj_in,
    first_in,
    second_in,
    proj_out,
    first_out,
    second_out,
):
    groups = lax.axis_size("grp")
    members = lax.axis_size("dev")
    slot_count = groups * members
    everyone = ("grp", "dev")
    tok_count = tokens.shape[0]
    capacity = 3 * tok_count // slot_count
    pair = 2 * capacity
    pair_rows = slot_count * pair

    my_group = lax.axis_index("grp")
    group_expert = lax.dynamic_slice_in_dim(slot_expert, my_group * members, members)
    group_expert = jnp.clip(group_expert, 0, E - 1)
    low_out = proj_out.astype(jnp.bfloat16)
    all_down = lax.all_gather(low_out, "grp", axis=0, tiled=True)
    low_in = proj_in.astype(jnp.bfloat16)
    all_up = lax.all_gather(low_in, "grp", axis=0, tiled=True)

    flat_target = targets.reshape(-1)
    onehot = (flat_target[:, None] == jnp.arange(slot_count, dtype=jnp.int32)[None, :]).astype(
        jnp.int32
    )
    earlier = jnp.cumsum(onehot, axis=0) - onehot
    position = jnp.sum(earlier * onehot, axis=1)
    within = position < capacity
    row = jnp.where(within, flat_target * pair + position, -pair_rows).reshape(tok_count, 2)
    row_x = [row[:, 0], row[:, 1]]
    row_dy = [row[:, 0] + capacity, row[:, 1] + capacity]
    places = jnp.arange(pair_rows, dtype=jnp.int32)

    hit_x = (places[:, None] == row_x[0][None, :]) | (places[:, None] == row_x[1][None, :])
    hit_0 = places[:, None] == row_dy[0][None, :]
    hit_1 = places[:, None] == row_dy[1][None, :]
    picker = jnp.concatenate([hit_x, hit_0, hit_1], axis=1).astype(jnp.bfloat16)
    cot_float = cotangent.astype(jnp.float32)
    scaled = [(route_weight[:, k : k + 1] * cot_float).astype(jnp.bfloat16) for k in (0, 1)]
    source = jnp.concatenate([tokens] + scaled, axis=0)
    send = jnp.dot(picker, source, preferred_element_type=jnp.float32).astype(jnp.bfloat16)
    slot_both = exchange(send.reshape(slot_count, pair, D), everyone)

    got_down = exchange(after(pick_experts(all_down, group_expert), slot_both), "dev")
    got_up = exchange(after(pick_experts(all_up, group_expert), got_down), "dev")
    slot_x = slot_both[:, :capacity].reshape(slot_count * capacity, D)
    slot_dy = slot_both[:, capacity:].reshape(slot_count * capacity, D)
    slot_up = got_up.reshape(D, 2 * FF)
    slot_down = got_down.reshape(FF, D)
    result, rows_dx, grad_up, grad_down = slot_pass(slot_x, slot_dy, slot_up, slot_down)

    rows_up = exchange(grad_up.reshape(members, D // members, 2 * FF), "dev")
    part_up = expert_sums(group_expert, rows_up)
    back = jnp.concatenate(
        [result.reshape(slot_count, capacity, D), rows_dx.reshape(slot_count, capacity, D)],
        axis=1,
    )
    down_ready = after(grad_down.reshape(members, FF // members, D), part_up, back)
    rows_down = exchange(down_ready, "dev")
    back = exchange(after(back, rows_down), everyone).reshape(pair_rows, D)

    part_down = expert_sums(group_expert, rows_down)
    sum_up = lax.psum_scatter(part_up, "grp", scatter_dimension=0, tiled=True)
    sum_down = lax.psum_scatter(part_down, "grp", scatter_dimension=0, tiled=True)

    take_0 = row_x[0][:, None] == places[None, :]
    take_1 = row_x[1][:, None] == places[None, :]
    take_dx = (row_dy[0][:, None] == places[None, :]) | (row_dy[1][:, None] == places[None, :])
    taker = jnp.concatenate([take_0, take_1, take_dx], axis=0).astype(jnp.bfloat16)
    taken = jnp.dot(taker, back, preferred_element_type=jnp.float32)
    out_0 = taken[:tok_count]
    out_1 = taken[tok_count : 2 * tok_count]
    mixed = (route_weight[:, 0:1] * out_0 + route_weight[:, 1:2] * out_1).astype(jnp.bfloat16)
    token_grad = taken[2 * tok_count :].astype(jnp.bfloat16)
    mix_grad = jnp.stack(
        [jnp.sum(cot_float * out_0, axis=1), jnp.sum(cot_float * out_1, axis=1)], axis=1
    )

    trained_in, mean_in, square_in = adam_step(
        proj_in, first_in, second_in, sum_up.astype(jnp.float32)
    )
    trained_out, mean_out, square_out = adam_step(
        proj_out, first_out, second_out, sum_down.astype(jnp.float32)
    )
    return (
        mixed,
        token_grad,
        mix_grad,
        trained_in,
        mean_in,
        square_in,
        trained_out,
        mean_out,
        square_out,
    )


def solution(mesh):
    in_specs = (
        P(("grp", "dev"), None),
        P(("grp", "dev"), None),
        P(("grp", "dev"), None),
        P(),
        P(("grp", "dev"), None),
        P("grp", "dev", None),
        P("grp", "dev", None),
        P("grp", "dev", None),
        P("grp", "dev", None),
        P("grp", "dev", None),
        P("grp", "dev", None),
    )
    out_specs = (
        P(("grp", "dev"), None),
        P(("grp", "dev"), None),
        P(("grp", "dev"), None),
        P("grp", "dev", None),
        P("grp", "dev", None),
        P("grp", "dev", None),
        P("grp", "dev", None),
        P("grp", "dev", None),
        P("grp", "dev", None),
    )
    return jax.shard_map(
        on_device, mesh=mesh, in_specs=in_specs, out_specs=out_specs, check_vma=False
    )
```

time: 1170 us -> 987 us (0.84)
  blocking collectives: 435 us -> 98.2 us
  waiting for transfers between devices: 484 us -> 691 us
  local copies, waits for them, and re-layouts: 88.7 us -> 42.2 us
  Pallas kernels: 0 us -> 17.4 us
  other arithmetic: 63.1 us -> 47.7 us
    all_to_all x4 -> x1, blocking collectives: 435 us -> 98.2 us  [exchange(): lax.all_to_all(payload, axes, split_axis=0, concat_axis=0, tiled=True)]
    all_to_all x4 -> x5, waiting for transfers between devices: 252 us -> 390 us  [exchange(): lax.all_to_all(payload, axes, split_axis=0, concat_axis=0, tiled=True)]
    all_gather x2, waiting for transfers between devices: 128 us -> 171 us  [the longest x1 95.8 us: on_device(): all_up = lax.all_gather(low_in, 'grp', axis=0, tiled=True)]
    convert_element_type x3 -> x0, local copies, waits for them, and re-layouts: 34.8 us -> none  [the longest x1 20.9 us: on_device(): part_up.astype(jnp.bfloat16)]
    reduce_scatter x2, waiting for transfers between devices: 104 us -> 130 us  [the longest x1 117 us: on_device(): sum_up = lax.psum_scatter(part_up, 'grp', scatter_dimension=0, tiled=True)]
    dot_general x2, matrix products: 23.2 us -> 4.86 us  [the longest x1 3.47 us: on_device(): jnp.dot(picker, source, preferred_element_type=jnp.float32)]
    pallas_call x0 -> x2, Pallas kernels: none -> 17.4 us  [expert_sums(): pl.pallas_call(kernel, grid_spec=pltpu.PrefetchScalarGridSpec(num_scalar_...]
    gather x10 -> x2, local copies, waits for them, and re-layouts: 34 us -> 16.8 us  [pick_experts(): return jnp.take(stack, experts, axis=0, mode='clip')]
  transfers between devices with their start and end apart: 8 -> 9, of which waited for: 7 -> 7; matrix products, arithmetic and copies ran while one was open for 7% -> 8% of each run, Pallas kernels for 0% -> 0%
where the time goes in v1:
time: 987 us; the launch traced here: 984 us
  waiting for transfers between devices  691 us (70%)
  blocking collectives  98.2 us (10%)
  other arithmetic  47.7 us (5%)
  matrix products  42.6 us (4%)
  local copies, waits for them, and re-layouts  42.2 us (4%)
  starting transfers between devices  31.2 us (3%)
  Pallas kernels  17.4 us (2%)
  between operations  14 us (1%)
    all_to_all x5, waiting for transfers between devices, exchange(): lax.all_to_all(payload, axes, split_axis=0, concat_axis=0, tiled=True)  390 us
    reduce_scatter x1, waiting for transfers between devices, on_device(): sum_up = lax.psum_scatter(part_up, 'grp', scatter_dimension=0, tiled=True)  117 us
    all_to_all x1, blocking collectives, exchange(): lax.all_to_all(payload, axes, split_axis=0, concat_axis=0, tiled=True)  98.2 us
    all_gather x1, waiting for transfers between devices, on_device(): all_up = lax.all_gather(low_in, 'grp', axis=0, tiled=True)  95.8 us
    all_gather x1, waiting for transfers between devices, on_device(): all_down = lax.all_gather(low_out, 'grp', axis=0, tiled=True)  74.8 us
    all_to_all x5, starting transfers between devices, exchange(): lax.all_to_all(payload, axes, split_axis=0, concat_axis=0, tiled=True)  31.1 us
    sub x2, other arithmetic, adam_step(): return (weight - learn_rate * update, new_moment, new_square)  30 us
  transfers between devices with their start and end apart: 9, of which 7 were waited for; matrix products, arithmetic and copies ran while one was open for 8% of the time, Pallas kernels for 0%

profile of v1, /device:TPU:10, one launch (start us, length us, event | category | flops | bytes accessed | tf_op | source)
XLA Modules:
  0.0 984.0 jit_solution(12675853973303007928)
XLA Ops:
  11.1 6.1 convert_element_type.59
  23.4 6.0 all-to-all-start
  29.5 74.8 %all-gather.5.cloned.1.call-done = bf16[16,128,2048]{2,1,0:T(8,128)(2,1)} async-done(((bf16[4,128,2048]{2,1,0:T(8,128)(2,1)}), bf16[16,128,2048]{2,1,0:T(8,128)(2,1)}) %all-gather.5.cloned.1.call-update) | async-done | bytes 8388624 | tf_op jit(solution)/shard_map/all_gather | solution.py:134
  104.3 6.2 gather_fusion.1
  110.5 6.0 all-to-all-start.1
  116.6 95.8 %all-gather.3.cloned.1.call-done = bf16[16,256,2048]{2,1,0:T(8,128)(2,1)} async-done(((bf16[4,256,2048]{2,1,0:T(8,128)(2,1)}), bf16[16,256,2048]{2,1,0:T(8,128)(2,1)}) %all-gather.3.cloned.1.call-update) | async-done | bytes 16777232 | tf_op jit(solution)/shard_map/all_gather | solution.py:136
  212.4 10.6 %gather_fusion = bf16[8,256,2048]{2,1,0:T(8,128)(2,1)} fusion(bf16[16,256,2048]{2,1,0:T(8,128)(2,1)} %all-gather.3.cloned.1.call-done, s32[1024]{0:T(1024)S(1)} %pad_clamp_fusion), kind=kCustom, calls=%fused_computation | custom fusion | bytes 16777248 | tf_op jit(solution)/shard_map/jit(_take)/gather | solution.py:101
  223.0 6.0 all-to-all-start.2
  237.1 172.1 %all-to-all-done.2 = bf16[8,256,2048]{2,1,0:T(8,128)(2,1)} async-done(((bf16[8,256,2048]{2,1,0:T(8,128)(2,1)}), bf16[8,256,2048]{2,1,0:T(8,128)(2,1)}, u32[]{:S(2)}, u32[]{:S(2)}) %all-to-all-start.2) | async-done | bytes 8388640 | tf_op jit(solution)/shard_map/all_to_all | solution.py:105
  409.2 6.4 fusion.41
  420.3 6.9 convolution_convert_fusion
  427.3 8.2 all-to-all-start.3
  435.5 10.2 %convolution_convert_fusion.3 = bf16[384,2048]{1,0:T(8,128)(2,1)} fusion(bf16[2048,2048]{1,0:T(8,128)(2,1)} %bitcast.8, bf16[384,1024]{1,0:T(8,128)(2,1)S(1)} %get-tuple-element.26, bf16[384,1024]{1,0:T(8,128)(2,1)S(1)} %get-tuple-element.25), kind=kOutput, calls=%fused_computation.16 | convolution fusion | flops 3225157632 | bytes 11534336 | tf_op jit(solution)/shard_map/dot_general | solution.py:40
  448.0 5.1 convolution_convert_fusion.4
  465.5 149.3 %all-to-all-done.3.rows_ref = bf16[8,256,2048]{2,1,0:T(8,128)(2,1)} async-done(((bf16[8,256,2048]{2,1,0:T(8,128)(2,1)}), bf16[8,256,2048]{2,1,0:T(8,128)(2,1)}, u32[]{:S(2)}, u32[]{:S(2)}) %all-to-all-start.3) | async-done | bytes 8388640 | tf_op jit(solution)/shard_map/all_to_all | solution.py:105
  614.8 13.1 %shard_map.178 = bf16[16,256,2048]{2,1,0:T(8,128)(2,1)S(1)} custom-call(s32[8]{0:T(128)S(1)} %dynamic-slice_clamp_fusion.expert_ref, bf16[8,256,2048]{2,1,0:T(8,128)(2,1)} %all-to-all-done.3.rows_ref), custom_call_target="tpu_custom_call" | custom-call | flops 4194304 | bytes 25165824 | tf_op jit(solution)/shard_map/pallas_call | solution.py:81
  627.9 5.7 copy-done
  633.6 98.2 %all_to_all.30.rows_ref = bf16[8,128,2048]{2,1,0:T(8,128)(2,1)S(1)} all-to-all(bf16[8,128,2048]{2,1,0:T(8,128)(2,1)} %bitcast.55), channel_id=1, replica_groups=mesh['grp'=4,'dev'=8] {'dev'}, dimensions={0} | all-to-all | bytes 8388608 | tf_op jit(solution)/shard_map/all_to_all | solution.py:105
  740.1 4.8 all-to-all-start.5
  745.2 68.2 %all-to-all-done.5 = bf16[32,24,2048]{2,1,0:T(8,128)(2,1)S(1)} async-done(((bf16[32,24,2048]{2,1,0:T(8,128)(2,1)}), bf16[32,24,2048]{2,1,0:T(8,128)(2,1)S(1)}, u32[]{:S(2)}, u32[]{:S(2)}) %all-to-all-start.5) | async-done | bytes 3145760 | tf_op jit(solution)/shard_map/all_to_all | solution.py:105
  817.6 13.3 %reduce-scatter.5.cloned.1.call-done = bf16[4,128,2048]{2,1,0:T(8,128)(2,1)} async-done(((bf16[16,128,2048]{2,1,0:T(8,128)(2,1)}), bf16[4,128,2048]{2,1,0:T(8,128)(2,1)}) %reduce-scatter.5.cloned.1.call-update) | async-done | bytes 2097168 | tf_op jit(solution)/shard_map/reduce_scatter | solution.py:180
  830.9 9.9 %multiply_subtract_fusion.1 = (f32[4,128,2048]{2,1,0:T(8,128)}, f32[4,128,2048]{2,1,0:T(8,128)}, f32[4,128,2048]{2,1,0:T(8,128)}) fusion(f32[4,128,2048]{2,1,0:T(8,128)} %param.19, bf16[4,128,2048]{2,1,0:T(8,128)(2,1)} %reduce-scatter.5.cloned.1.call-done, f32[4,128,2048]{2,1,0:T(8,128)} %param.20, f32[4,128,2048]{2,1,0:T(8,128)} %param.21), kind=kLoop, calls=%fused_computation.12 | loop fusion | flops 16777216 | bytes 27262976 | tf_op jit(solution)/shard_map/sub | solution.py:59
  840.8 116.6 %reduce-scatter.3.cloned.1.call-done = bf16[4,256,2048]{2,1,0:T(8,128)(2,1)} async-done(((bf16[16,256,2048]{2,1,0:T(8,128)(2,1)}), bf16[4,256,2048]{2,1,0:T(8,128)(2,1)}) %reduce-scatter.3.cloned.1.call-update) | async-done | bytes 4194320 | tf_op jit(solution)/shard_map/reduce_scatter | solution.py:179
  957.4 20.0 %multiply_subtract_fusion = (f32[4,256,2048]{2,1,0:T(8,128)}, f32[4,256,2048]{2,1,0:T(8,128)}, f32[4,256,2048]{2,1,0:T(8,128)}) fusion(f32[4,256,2048]{2,1,0:T(8,128)} %param.16, bf16[4,256,2048]{2,1,0:T(8,128)(2,1)} %reduce-scatter.3.cloned.1.call-done, f32[4,256,2048]{2,1,0:T(8,128)} %param.17, f32[4,256,2048]{2,1,0:T(8,128)} %param.18), kind=kLoop, calls=%fused_computation.6 | loop fusion | flops 33554432 | bytes 54525952 | tf_op jit(solution)/shard_map/sub | solution.py:59
  (70 shorter events, 50.3 us)
Async XLA Ops:
  7.2 97.2 %all-gather.5.cloned.1.call-start = ((), (), s32[]{:S(2)}) async-start(), calls=%async_computation.9 | async-start | bytes 10485760 | tf_op jit(solution)/shard_map/all_gather | solution.py:134
  11.1 201.3 %all-gather.3.cloned.1.call-start = ((), (), s32[]{:S(2)}) async-start(), calls=%async_computation.8 | async-start | bytes 20971520 | tf_op jit(solution)/shard_map/all_gather | solution.py:136
  17.2 0.7 copy-start.8
  17.2 2.2 copy-start.9
  17.2 2.5 copy-start.3
  17.2 2.7 copy-start.10
  23.4 6.0 copy-start.11
  23.4 87.1 %all-to-all-start = ((bf16[32,24,2048]{2,1,0:T(8,128)(2,1)}), bf16[32,24,2048]{2,1,0:T(8,128)(2,1)S(1)}, u32[]{:S(2)}, u32[]{:S(2)}) async-start(bf16[32,24,2048]{2,1,0:T(8,128)(2,1)} %bitcast.56), calls=%async_computation | async-start | bytes 6291456 | tf_op jit(solution)/shard_map/all_to_all | solution.py:105
  110.5 112.5 %all-to-all-start.1 = ((bf16[8,128,2048]{2,1,0:T(8,128)(2,1)}), bf16[8,128,2048]{2,1,0:T(8,128)(2,1)}, u32[]{:S(2)}, u32[]{:S(2)}) async-start(bf16[8,128,2048]{2,1,0:T(8,128)(2,1)} %gather_fusion.1), calls=%async_computation.1 | async-start | bytes 8388608 | tf_op jit(solution)/shard_map/all_to_all | solution.py:105
  223.0 186.2 %all-to-all-start.2 = ((bf16[8,256,2048]{2,1,0:T(8,128)(2,1)}), bf16[8,256,2048]{2,1,0:T(8,128)(2,1)}, u32[]{:S(2)}, u32[]{:S(2)}) async-start(bf16[8,256,2048]{2,1,0:T(8,128)(2,1)} %gather_fusion), calls=%async_computation.2 | async-start | bytes 16777216 | tf_op jit(solution)/shard_map/all_to_all | solution.py:105
  232.0 3.8 copy-start.2
  409.2 6.4 copy-start.5
  415.6 4.7 copy-start.7
  427.3 187.5 %all-to-all-start.3 = ((bf16[8,256,2048]{2,1,0:T(8,128)(2,1)}), bf16[8,256,2048]{2,1,0:T(8,128)(2,1)}, u32[]{:S(2)}, u32[]{:S(2)}) async-start(bf16[8,256,2048]{2,1,0:T(8,128)(2,1)} %bitcast.54), calls=%async_computation.3 | async-start | bytes 16777216 | tf_op jit(solution)/shard_map/all_to_all | solution.py:105
  435.5 395.4 %reduce-scatter.5.cloned.1.call-start = ((), (), s32[]{:S(2)}) async-start(), calls=%async_computation.11 | async-start | bytes 10485760 | tf_op jit(solution)/shard_map/reduce_scatter | solution.py:180
  456.7 4.3 copy-start.6
  627.9 5.7 copy-start
  736.1 3.4 copy-start.1
  739.5 217.9 %reduce-scatter.3.cloned.1.call-start = ((), (), s32[]{:S(2)}) async-start(), calls=%async_computation.10 | async-start | bytes 20971520 | tf_op jit(solution)/shard_map/reduce_scatter | solution.py:179
  740.1 73.3 %all-to-all-start.5 = ((bf16[32,24,2048]{2,1,0:T(8,128)(2,1)}), bf16[32,24,2048]{2,1,0:T(8,128)(2,1)S(1)}, u32[]{:S(2)}, u32[]{:S(2)}) async-start(bf16[32,24,2048]{2,1,0:T(8,128)(2,1)} %pad_maximum_fusion), calls=%async_computation.5 | async-start | bytes 6291456 | tf_op jit(solution)/shard_map/all_to_all | solution.py:105
  813.4 2.3 copy-start.4
Sparse Core Ops, SparseCore 0:
  11.2 93.0 all-gather.4
  106.5 105.8 all-gather.2
  739.6 91.2 reduce-scatter.4
  833.3 124.0 reduce-scatter.2

commit v2 on v1

--- a/solution.py
+++ b/solution.py
@@ -22,31 +22,6 @@
 def silu_parts(values):
     logistic = jax.nn.sigmoid(values)
     return (values * logistic, logistic * (1.0 + values * (1.0 - logistic)))
-
-
-def slot_pass(rows_x, rows_dy, weight_up, weight_down):
-    gate_up = jnp.dot(rows_x, weight_up, preferred_element_type=jnp.float32)
-    gating = gate_up[:, :FF]
-    upward = gate_up[:, FF:]
-    active, derivative = silu_parts(gating)
-    hidden = (active * upward).astype(jnp.bfloat16)
-    result = jnp.dot(hidden, weight_down, preferred_element_type=jnp.float32).astype(jnp.bfloat16)
-    dhidden = lax.dot_general(
-        rows_dy, weight_down, (((1,), (1,)), ((), ())), preferred_element_type=jnp.float32
-    )
-    grad_gateup = jnp.concatenate([dhidden * upward * derivative, dhidden * active], axis=1).astype(
-        jnp.bfloat16
-    )
-    rows_dx = lax.dot_general(
-        grad_gateup, weight_up, (((1,), (1,)), ((), ())), preferred_element_type=jnp.float32
-    ).astype(jnp.bfloat16)
-    grad_up = lax.dot_general(
-        rows_x, grad_gateup, (((0,), (0,)), ((), ())), preferred_element_type=jnp.float32
-    ).astype(jnp.bfloat16)
-    grad_down = lax.dot_general(
-        hidden, rows_dy, (((0,), (0,)), ((), ())), preferred_element_type=jnp.float32
-    ).astype(jnp.bfloat16)
-    return (result, rows_dx, grad_up, grad_down)
 
 
 def adam_step(weight, moment, square, gradient):
@@ -133,7 +108,9 @@
     low_out = proj_out.astype(jnp.bfloat16)
     all_down = lax.all_gather(low_out, "grp", axis=0, tiled=True)
     low_in = proj_in.astype(jnp.bfloat16)
-    all_up = lax.all_gather(low_in, "grp", axis=0, tiled=True)
+    half = low_in.shape[1] // 2
+    all_1 = lax.all_gather(low_in[:, :half], "grp", axis=0, tiled=True)
+    all_2 = lax.all_gather(low_in[:, half:], "grp", axis=0, tiled=True)
 
     flat_target = targets.reshape(-1)
     onehot = (flat_target[:, None] == jnp.arange(slot_count, dtype=jnp.int32)[None, :]).astype(
@@ -158,26 +135,63 @@
     slot_both = exchange(send.reshape(slot_count, pair, D), everyone)
 
     got_down = exchange(after(pick_experts(all_down, group_expert), slot_both), "dev")
-    got_up = exchange(after(pick_experts(all_up, group_expert), got_down), "dev")
-    slot_x = slot_both[:, :capacity].reshape(slot_count * capacity, D)
-    slot_dy = slot_both[:, capacity:].reshape(slot_count * capacity, D)
-    slot_up = got_up.reshape(D, 2 * FF)
+    got_1 = exchange(after(pick_experts(all_1, group_expert), got_down), "dev")
+    got_2 = exchange(after(pick_experts(all_2, group_expert), got_1), "dev")
+    slot_rows = slot_count * capacity
+    slot_x = slot_both[:, :capacity].reshape(slot_rows, D)
+    slot_dy = slot_both[:, capacity:].reshape(slot_rows, D)
+    split_x = slot_x.reshape(slot_rows, members, 2, half)
+    x_1 = split_x[:, :, 0].reshape(slot_rows, members * half)
+    x_2 = split_x[:, :, 1].reshape(slot_rows, members * half)
+    up_1 = got_1.reshape(members * half, 2 * FF)
+    up_2 = got_2.reshape(members * half, 2 * FF)
     slot_down = got_down.reshape(FF, D)
-    result, rows_dx, grad_up, grad_down = slot_pass(slot_x, slot_dy, slot_up, slot_down)
-
-    rows_up = exchange(grad_up.reshape(members, D // members, 2 * FF), "dev")
-    part_up = expert_sums(group_expert, rows_up)
+
+    across = (((1,), (1,)), ((), ()))
+    down = (((0,), (0,)), ((), ()))
+    dhidden = lax.dot_general(slot_dy, slot_down, across, preferred_element_type=jnp.float32)
+    gate_up = jnp.dot(x_1, up_1, preferred_element_type=jnp.float32) + jnp.dot(
+        x_2, up_2, preferred_element_type=jnp.float32
+    )
+    gating = gate_up[:, :FF]
+    upward = gate_up[:, FF:]
+    active, derivative = silu_parts(gating)
+    hidden = (active * upward).astype(jnp.bfloat16)
+    grad_gateup = jnp.concatenate([dhidden * upward * derivative, dhidden * active], axis=1).astype(
+        jnp.bfloat16
+    )
+
+    def low_dot(a, b, dims):
+        return lax.dot_general(a, b, dims, preferred_element_type=jnp.float32).astype(jnp.bfloat16)
+
+    grad_1 = low_dot(x_1, grad_gateup, down).reshape(members, half, 2 * FF)
+    rows_1 = exchange(grad_1, "dev")
+    grad_2 = low_dot(x_2, grad_gateup, down).reshape(members, half, 2 * FF)
+    grad_down = low_dot(hidden, slot_dy, down).reshape(members, FF // members, D)
+    result = low_dot(hidden, slot_down, (((1,), (0,)), ((), ())))
+    dx_1 = low_dot(grad_gateup, up_1, across)
+    dx_2 = low_dot(grad_gateup, up_2, across)
+    rows_dx = jnp.stack(
+        [dx_1.reshape(slot_rows, members, half), dx_2.reshape(slot_rows, members, half)],
+        axis=2,
+    ).reshape(slot_rows, D)
     back = jnp.concatenate(
-        [result.reshape(slot_count, capacity, D), rows_dx.reshape(slot_count, capacity, D)],
+        [
+            result.reshape(slot_count, capacity, D),
+            rows_dx.reshape(slot_count, capacity, D),
+        ],
         axis=1,
     )
-    down_ready = after(grad_down.reshape(members, FF // members, D), part_up, back)
-    rows_down = exchange(down_ready, "dev")
+    rows_2 = exchange(after(grad_2, rows_1), "dev")
+    rows_down = exchange(after(grad_down, rows_2, back), "dev")
     back = exchange(after(back, rows_down), everyone).reshape(pair_rows, D)
-
+    part_1 = expert_sums(group_expert, rows_1)
+    part_2 = expert_sums(group_expert, rows_2)
     part_down = expert_sums(group_expert, rows_down)
-    sum_up = lax.psum_scatter(part_up, "grp", scatter_dimension=0, tiled=True)
+    sum_1 = lax.psum_scatter(part_1, "grp", scatter_dimension=0, tiled=True)
+    sum_2 = lax.psum_scatter(part_2, "grp", scatter_dimension=0, tiled=True)
     sum_down = lax.psum_scatter(part_down, "grp", scatter_dimension=0, tiled=True)
+    sum_up = jnp.concatenate([sum_1, sum_2], axis=1)
 
     take_0 = row_x[0][:, None] == places[None, :]
     take_1 = row_x[1][:, None] == places[None, :]

time: 987 us -> 895 us (0.907)
  waiting for transfers between devices: 691 us -> 374 us
  blocking collectives: 98.2 us -> 291 us
  local copies, waits for them, and re-layouts: 42.2 us -> 66.9 us
    all_to_all x1 -> x3, blocking collectives: 98.2 us -> 291 us  [exchange(): lax.all_to_all(payload, axes, split_axis=0, concat_axis=0, tiled=True)]
    all_to_all x5, waiting for transfers between devices: 390 us -> 240 us  [exchange(): lax.all_to_all(payload, axes, split_axis=0, concat_axis=0, tiled=True)]
    reduce_scatter x1 -> x2, waiting for transfers between devices: 117 us -> 0.01 us  [the longest x1 0.01 us: on_device(): sum_1 = lax.psum_scatter(part_1, 'grp', scatter_dimension=0, tiled=True)]
    all_gather x1 -> x2, waiting for transfers between devices: 95.8 us -> 57.9 us  [the longest x1 47.5 us: on_device(): all_1 = lax.all_gather(low_in[:, :half], 'grp', axis=0, tiled=True)]
    slice x2 -> x6, local copies, waits for them, and re-layouts: 3.1 us -> 18.3 us  [the longest x2 8.08 us: on_device(): x_2 = split_x[:, :, 1].reshape(slot_rows, members * half)]
    reduce_scatter x1, waiting for transfers between devices: 13.3 us -> 0.01 us  [on_device(): lax.psum_scatter(part_down, 'grp', scatter_dimension=0, tiled=True)]
    another operation x1 -> x5, local copies, waits for them, and re-layouts: 0.01 us -> 12.4 us  [the longest x1 4.3 us: on_device(): split_x = slot_x.reshape(slot_rows, members, 2, half)]
    dot_general x6 -> x9, matrix products: 37.7 us -> 37 us  [the longest x6 22.7 us: low_dot(): lax.dot_general(a, b, dims, preferred_element_type=jnp.float32)]
  transfers between devices with their start and end apart: 9 -> 11, of which waited for: 7 -> 7; matrix products, arithmetic and copies ran while one was open for 8% -> 14% of each run, Pallas kernels for 0% -> 1%
where the time goes in v2:
time: 895 us; the launch traced here: 884 us
  waiting for transfers between devices  374 us (42%)
  blocking collectives  291 us (33%)
  local copies, waits for them, and re-layouts  66.9 us (7%)
  other arithmetic  49 us (5%)
  matrix products  41.8 us (5%)
  starting transfers between devices  33.8 us (4%)
  between operations  14.7 us (2%)
  Pallas kernels  12.9 us (1%)
    all_to_all x3, blocking collectives, exchange(): lax.all_to_all(payload, axes, split_axis=0, concat_axis=0, tiled=True)  291 us
    all_to_all x5, waiting for transfers between devices, exchange(): lax.all_to_all(payload, axes, split_axis=0, concat_axis=0, tiled=True)  240 us
    all_gather x1, waiting for transfers between devices, on_device(): all_down = lax.all_gather(low_out, 'grp', axis=0, tiled=True)  75.2 us
    all_gather x1, waiting for transfers between devices, on_device(): all_1 = lax.all_gather(low_in[:, :half], 'grp', axis=0, tiled=True)  47.5 us
    all_to_all x5, starting transfers between devices, exchange(): lax.all_to_all(payload, axes, split_axis=0, concat_axis=0, tiled=True)  33 us
    sub x2, other arithmetic, adam_step(): return (weight - learn_rate * update, new_moment, new_square)  28.8 us
    dot_general x6, matrix products, low_dot(): lax.dot_general(a, b, dims, preferred_element_type=jnp.float32)  22.7 us
    gather x3, local copies, waits for them, and re-layouts, pick_experts(): return jnp.take(stack, experts, axis=0, mode='clip')  18.6 us
  transfers between devices with their start and end apart: 11, of which 7 were waited for; matrix products, arithmetic and copies ran while one was open for 14% of the time, Pallas kernels for 1%

profile of v2, /device:TPU:10, one launch (start us, length us, event | category | flops | bytes accessed | tf_op | source)
XLA Modules:
  0.0 883.7 jit_solution(8023191074656195466)
XLA Ops:
  23.1 6.0 all-to-all-start
  29.2 75.2 %all-gather.6.cloned.1.call-done = bf16[16,128,2048]{2,1,0:T(8,128)(2,1)} async-done(((bf16[4,128,2048]{2,1,0:T(8,128)(2,1)}), bf16[16,128,2048]{2,1,0:T(8,128)(2,1)}) %all-gather.6.cloned.1.call-update) | async-done | bytes 8388624 | tf_op jit(solution)/shard_map/all_gather | solution.py:109
  104.4 6.2 gather_fusion.1
  110.6 6.0 all-to-all-start.1
  117.4 47.5 %all-gather.4.cloned.1.call-done = bf16[16,128,2048]{2,1,0:T(8,128)(2,1)} async-done(((bf16[4,128,2048]{2,1,0:T(8,128)(2,1)}), bf16[16,128,2048]{2,1,0:T(8,128)(2,1)}) %all-gather.4.cloned.1.call-update) | async-done | bytes 8388624 | tf_op jit(solution)/shard_map/all_gather | solution.py:112
  164.8 6.2 gather_fusion
  171.1 35.9 %all-to-all-done.1 = bf16[8,128,2048]{2,1,0:T(8,128)(2,1)} async-done(((bf16[8,128,2048]{2,1,0:T(8,128)(2,1)}), bf16[8,128,2048]{2,1,0:T(8,128)(2,1)}, u32[]{:S(2)}, u32[]{:S(2)}) %all-to-all-start.1) | async-done | bytes 4194336 | tf_op jit(solution)/shard_map/all_to_all | solution.py:80
  207.0 7.8 all-to-all-start.2
  214.8 10.4 %all-gather.8.cloned.1.call-done = bf16[16,128,2048]{2,1,0:T(8,128)(2,1)} async-done(((bf16[4,128,2048]{2,1,0:T(8,128)(2,1)}), bf16[16,128,2048]{2,1,0:T(8,128)(2,1)}) %all-gather.8.cloned.1.call-update) | async-done | bytes 8388624 | tf_op jit(solution)/shard_map/all_gather | solution.py:113
  225.3 6.2 gather_fusion.2
  231.5 72.8 %all-to-all-done.2 = bf16[8,128,2048]{2,1,0:T(8,128)(2,1)} async-done(((bf16[8,128,2048]{2,1,0:T(8,128)(2,1)}), bf16[8,128,2048]{2,1,0:T(8,128)(2,1)}, u32[]{:S(2)}, u32[]{:S(2)}) %all-to-all-start.2) | async-done | bytes 4194336 | tf_op jit(solution)/shard_map/all_to_all | solution.py:80
  304.3 7.9 all-to-all-start.3
  323.3 4.8 copy.53
  338.4 63.0 %all-to-all-done.3 = bf16[8,128,2048]{2,1,0:T(8,128)(2,1)} async-done(((bf16[8,128,2048]{2,1,0:T(8,128)(2,1)}), bf16[8,128,2048]{2,1,0:T(8,128)(2,1)}, u32[]{:S(2)}, u32[]{:S(2)}) %all-to-all-start.3) | async-done | bytes 4194336 | tf_op jit(solution)/shard_map/all_to_all | solution.py:80
  406.0 5.5 multiply_convert_fusion.1
  413.8 98.0 %all_to_all.40.rows_ref = bf16[8,128,2048]{2,1,0:T(8,128)(2,1)S(1)} all-to-all(bf16[8,128,2048]{2,1,0:T(8,128)(2,1)S(1)} %bitcast.67), channel_id=1, replica_groups=mesh['grp'=4,'dev'=8] {'dev'}, dimensions={0} | all-to-all | bytes 8388608 | tf_op jit(solution)/shard_map/all_to_all | solution.py:80
  523.0 96.3 %all_to_all.41.rows_ref = bf16[8,128,2048]{2,1,0:T(8,128)(2,1)S(1)} all-to-all(bf16[8,128,2048]{2,1,0:T(8,128)(2,1)S(1)} %bitcast.68), channel_id=1, replica_groups=mesh['grp'=4,'dev'=8] {'dev'}, dimensions={0} | all-to-all | bytes 8388608 | tf_op jit(solution)/shard_map/all_to_all | solution.py:80
  632.0 5.5 convolution_convert_fusion.6
  649.4 6.0 convolution_convert_fusion.4
  665.8 96.4 %all_to_all.42.rows_ref = bf16[8,128,2048]{2,1,0:T(8,128)(2,1)S(1)} all-to-all(bf16[8,128,2048]{2,1,0:T(8,128)(2,1)S(1)} %bitcast.66), channel_id=1, replica_groups=mesh['grp'=4,'dev'=8] {'dev'}, dimensions={0} | all-to-all | bytes 8388608 | tf_op jit(solution)/shard_map/all_to_all | solution.py:80
  769.8 5.2 all-to-all-start.7
  775.4 68.2 %all-to-all-done.7 = bf16[32,24,2048]{2,1,0:T(8,128)(2,1)S(1)} async-done(((bf16[32,24,2048]{2,1,0:T(8,128)(2,1)}), bf16[32,24,2048]{2,1,0:T(8,128)(2,1)S(1)}, u32[]{:S(2)}, u32[]{:S(2)}) %all-to-all-start.7) | async-done | bytes 3145760 | tf_op jit(solution)/shard_map/all_to_all | solution.py:80
  847.8 18.9 %multiply_subtract_fusion = (f32[4,256,2048]{2,1,0:T(8,128)}, f32[4,256,2048]{2,1,0:T(8,128)}, f32[4,256,2048]{2,1,0:T(8,128)}) fusion(f32[4,256,2048]{2,1,0:T(8,128)} %param.16, bf16[4,128,2048]{2,1,0:T(8,128)(2,1)} %reduce-scatter.6.cloned.1.call-done, bf16[4,128,2048]{2,1,0:T(8,128)(2,1)} %reduce-scatter.4.cloned.1.call-done, f32[4,256,2048]{2,1,0:T(8,128)} %param.17, ...), kind=kLoop, calls=%fused_computation.7 | loop fusion | flops 39845888 | bytes 54525952 | tf_op jit(solution)/shard_map/sub | solution.py:34
  866.7 9.9 %multiply_subtract_fusion.1 = (f32[4,128,2048]{2,1,0:T(8,128)}, f32[4,128,2048]{2,1,0:T(8,128)}, f32[4,128,2048]{2,1,0:T(8,128)}) fusion(f32[4,128,2048]{2,1,0:T(8,128)} %param.19, bf16[4,128,2048]{2,1,0:T(8,128)(2,1)} %reduce-scatter.8.cloned.1.call-done, f32[4,128,2048]{2,1,0:T(8,128)} %param.20, f32[4,128,2048]{2,1,0:T(8,128)} %param.21), kind=kLoop, calls=%fused_computation.13 | loop fusion | flops 16777216 | bytes 27262976 | tf_op jit(solution)/shard_map/sub | solution.py:34
  (98 shorter events, 103.0 us)
Async XLA Ops:
  7.2 97.2 %all-gather.6.cloned.1.call-start = ((), (), s32[]{:S(2)}) async-start(), calls=%async_computation.12 | async-start | bytes 10485760 | tf_op jit(solution)/shard_map/all_gather | solution.py:109
  11.1 153.8 %all-gather.4.cloned.1.call-start = ((), (), s32[]{:S(2)}) async-start(), calls=%async_computation.11 | async-start | bytes 10485760 | tf_op jit(solution)/shard_map/all_gather | solution.py:112
  15.2 2.4 copy-start.10
  15.2 3.9 copy-start.11
  15.2 4.2 copy-start.6
  23.1 6.0 copy-start.13
  23.1 87.5 %all-to-all-start = ((bf16[32,24,2048]{2,1,0:T(8,128)(2,1)}), bf16[32,24,2048]{2,1,0:T(8,128)(2,1)S(1)}, u32[]{:S(2)}, u32[]{:S(2)}) async-start(bf16[32,24,2048]{2,1,0:T(8,128)(2,1)} %bitcast.69), calls=%async_computation | async-start | bytes 6291456 | tf_op jit(solution)/shard_map/all_to_all | solution.py:80
  110.6 96.4 %all-to-all-start.1 = ((bf16[8,128,2048]{2,1,0:T(8,128)(2,1)}), bf16[8,128,2048]{2,1,0:T(8,128)(2,1)}, u32[]{:S(2)}, u32[]{:S(2)}) async-start(bf16[8,128,2048]{2,1,0:T(8,128)(2,1)} %gather_fusion.1), calls=%async_computation.1 | async-start | bytes 8388608 | tf_op jit(solution)/shard_map/all_to_all | solution.py:80
  116.7 108.6 %all-gather.8.cloned.1.call-start = ((), (), s32[]{:S(2)}) async-start(), calls=%async_computation.13 | async-start | bytes 10485760 | tf_op jit(solution)/shard_map/all_gather | solution.py:113
  207.0 97.3 %all-to-all-start.2 = ((bf16[8,128,2048]{2,1,0:T(8,128)(2,1)}), bf16[8,128,2048]{2,1,0:T(8,128)(2,1)}, u32[]{:S(2)}, u32[]{:S(2)}) async-start(bf16[8,128,2048]{2,1,0:T(8,128)(2,1)} %gather_fusion), calls=%async_computation.2 | async-start | bytes 8388608 | tf_op jit(solution)/shard_map/all_to_all | solution.py:80
  304.3 97.1 %all-to-all-start.3 = ((bf16[8,128,2048]{2,1,0:T(8,128)(2,1)}), bf16[8,128,2048]{2,1,0:T(8,128)(2,1)}, u32[]{:S(2)}, u32[]{:S(2)}) async-start(bf16[8,128,2048]{2,1,0:T(8,128)(2,1)} %gather_fusion.2), calls=%async_computation.3 | async-start | bytes 8388608 | tf_op jit(solution)/shard_map/all_to_all | solution.py:80
  312.2 535.6 %reduce-scatter.4.cloned.1.call-start = ((), (), s32[]{:S(2)}) async-start(), calls=%async_computation.14 | async-start | bytes 10485760 | tf_op jit(solution)/shard_map/reduce_scatter | solution.py:191
  323.3 9.5 %copy-start.3 = (bf16[32,12,2048]{2,1,0:T(8,128)(2,1)S(1)}, bf16[32,12,2048]{2,1,0:T(8,128)(2,1)}, u32[]{:S(2)}) copy-start(bf16[32,12,2048]{2,1,0:T(8,128)(2,1)} %get-tuple-element.36) | copy-start | bytes 4718596
  401.4 4.5 copy-start.8
  405.9 5.5 copy-start.5
  411.5 215.8 %copy-start.15 = (bf16[384,1024]{1,0:T(8,128)(2,1)}, bf16[384,1024]{1,0:T(8,128)(2,1)S(1)}, u32[]{:S(2)}) copy-start(bf16[384,1024]{1,0:T(8,128)(2,1)S(1)} %get-tuple-element.30) | copy-start | bytes 2359300
  516.1 3.4 copy-start
  519.5 328.3 %reduce-scatter.6.cloned.1.call-start = ((), (), s32[]{:S(2)}) async-start(), calls=%async_computation.15 | async-start | bytes 10485760 | tf_op jit(solution)/shard_map/reduce_scatter | solution.py:192
  623.6 3.4 copy-start.1
  627.0 239.7 %reduce-scatter.8.cloned.1.call-start = ((), (), s32[]{:S(2)}) async-start(), calls=%async_computation.16 | async-start | bytes 10485760 | tf_op jit(solution)/shard_map/reduce_scatter | solution.py:193
  659.0 4.4 copy-start.9
  659.0 4.4 copy-start.14
  766.5 3.3 copy-start.2
  769.8 73.8 %all-to-all-start.7 = ((bf16[32,24,2048]{2,1,0:T(8,128)(2,1)}), bf16[32,24,2048]{2,1,0:T(8,128)(2,1)S(1)}, u32[]{:S(2)}, u32[]{:S(2)}) async-start(bf16[32,24,2048]{2,1,0:T(8,128)(2,1)} %pad_maximum_fusion.1), calls=%async_computation.7 | async-start | bytes 6291456 | tf_op jit(solution)/shard_map/all_to_all | solution.py:80
  (3 other events, 5.5 us)
Sparse Core Ops, SparseCore 0:
  11.2 93.1 all-gather.5
  106.5 58.2 all-gather.3
  167.0 58.2 all-gather.7
  519.7 71.1 reduce-scatter.3
  627.1 71.1 reduce-scatter.5
  770.0 91.0 reduce-scatter.7
